TPU v7x, 32 devices: a whole 2x2x4 slice. The times are simulated.
32 devices in a mesh: dp: 8 (over z, y), tensor: 4 (over x, core).
Axes of the slice: x: 2, y: 2, z: 4, core: 2. Of those that a mesh axis runs over, the one named last changes fastest.
Arguments:
- block_in: bfloat16 [16384, 768], P(('dp', 'tensor')), may hold values from -6 to 6
- enc_states: bfloat16 [65536, 768], P(('dp', 'tensor')), may hold values from -6 to 6
- dec_len: int32 [64], P('dp'), may hold values from 32 to 256
- enc_len: int32 [64], P('dp'), may hold values from 128 to 1024
- gain_self: bfloat16 [768], replicated, may hold values from 0.5 to 1.5
- self_query: bfloat16 [768, 768], P(None, 'tensor'), may hold values from -0.02734375 to 0.02734375
- self_key: bfloat16 [768, 768], P(None, 'tensor'), may hold values from -0.21875 to 0.21875
- self_value: bfloat16 [768, 768], P(None, 'tensor'), may hold values from -0.21875 to 0.21875
- self_out: bfloat16 [768, 768], P('tensor'), may hold values from -0.875 to 0.875
- rel_table: bfloat16 [32, 12], P(None, 'tensor'), may hold values from -4 to 4
- gain_cross: bfloat16 [768], replicated, may hold values from 0.5 to 1.5
- cross_query: bfloat16 [768, 768], P(None, 'tensor'), may hold values from -0.02734375 to 0.02734375
- cross_key: bfloat16 [768, 768], P(None, 'tensor'), may hold values from -0.21875 to 0.21875
- cross_value: bfloat16 [768, 768], P(None, 'tensor'), may hold values from -0.21875 to 0.21875
- cross_out: bfloat16 [768, 768], P('tensor'), may hold values from -0.875 to 0.875
- gain_ff: bfloat16 [768], replicated, may hold values from 0.5 to 1.5
- ff_in: bfloat16 [768, 3072], P(None, 'tensor'), may hold values from -0.21875 to 0.21875
- ff_out: bfloat16 [3072, 768], P('tensor'), may hold values from -0.109375 to 0.109375
- out_grad: bfloat16 [16384, 768], P(('dp', 'tensor')), may hold values from -6 to 6
Outputs:
- block_out: bfloat16 [16384, 768], P(('dp', 'tensor'))
- grad_in: float32 [16384, 768], P(('dp', 'tensor'))
- grad_enc: float32 [65536, 768], P(('dp', 'tensor'))
- grad_gain_self: float32 [768], replicated
- grad_self_query: float32 [768, 768], P(None, 'tensor')
- grad_self_key: float32 [768, 768], P(None, 'tensor')
- grad_self_value: float32 [768, 768], P(None, 'tensor')
- grad_self_out: float32 [768, 768], P('tensor')
- grad_rel_table: float32 [32, 12], P(None, 'tensor')
- grad_gain_cross: float32 [768], replicated
- grad_cross_query: float32 [768, 768], P(None, 'tensor')
- grad_cross_key: float32 [768, 768], P(None, 'tensor')
- grad_cross_value: float32 [768, 768], P(None, 'tensor')
- grad_cross_out: float32 [768, 768], P('tensor')
- grad_gain_ff: float32 [768], replicated
- grad_ff_in: float32 [768, 3072], P(None, 'tensor')
- grad_ff_out: float32 [3072, 768], P('tensor')
All inputs are finite; a program needn't handle non-finite values.
Results may differ from a plain program's by a relative error of at most 0.025.
Values may be sent and summed in bfloat16 or wider, within the bound.
No kernel may reach another device: no remote copies, remote signals or barrier semaphores. Data moves between devices by JAX's collectives and lax.ppermute only.
A program may use at most 256 MiB of HBM per device.

v0:
```python
import math
import jax
import jax.numpy as jnp
import numpy as np
from jax import lax
from jax.sharding import PartitionSpec as P

BUCKETS = 32
MAX_DIST = 128
LEN = 256
ENC = 1024
norm_eps = 1e-06
masked_score = -1000000000.0


def bucket_limits():
    half_count = BUCKETS // 2
    growth_ratio = MAX_DIST / half_count
    return np.array(
        [
            int(math.ceil(half_count * growth_ratio ** (level_index / half_count)))
            for level_index in range(1, half_count)
        ],
        dtype=np.int32,
    )


def bucket_onehot(length):
    places = jnp.arange(length, dtype=jnp.int32)
    distance = jnp.maximum(places[:, None] - places[None, :], 0)
    limits = jnp.asarray(bucket_limits())
    above_count = jnp.sum((distance[:, :, None] >= limits[None, None, :]).astype(jnp.int32), axis=2)
    half_count = BUCKETS // 2
    buckets = jnp.where(distance < half_count, distance, half_count + above_count)
    return (buckets[:, :, None] == jnp.arange(BUCKETS, dtype=jnp.int32)[None, None, :]).astype(
        jnp.float32
    )


def collect_rows(values):
    return lax.all_gather(values, "tensor", axis=0, tiled=True)


def spread_rows(values):
    return lax.psum_scatter(values, "tensor", scatter_dimension=0, tiled=True)


def rms_norm(values, scales):
    return values * lax.rsqrt(jnp.mean(values * values, axis=-1, keepdims=True) + norm_eps) * scales


def norm_back(values, scales, incoming):
    primal, pullback = jax.vjp(rms_norm, values, scales)
    return pullback(incoming)


def smooth_act(values):
    return jax.nn.gelu(values, approximate=True)


def act_back(values, incoming):
    primal, pullback = jax.vjp(smooth_act, values)
    return pullback(incoming)[0]


def matmul(former, latter):
    return jnp.dot(former, latter, preferred_element_type=jnp.float32)


def inner_rows(former, latter):
    return lax.dot_general(
        former, latter, (((0,), (0,)), ((), ())), preferred_element_type=jnp.float32
    )


def times_transposed(former, latter):
    return lax.dot_general(
        former, latter, (((1,), (1,)), ((), ())), preferred_element_type=jnp.float32
    )


def attend_forward(query_rows, key_rows, value_rows, extra_bias, allowed):
    scores = (
        jnp.einsum("sqhd,skhd->shqk", query_rows, key_rows, preferred_element_type=jnp.float32)
        + extra_bias
    )
    scores = jnp.where(allowed, scores, masked_score)
    top_score = jnp.max(scores, axis=-1, keepdims=True)
    weights = jnp.exp(scores - top_score)
    totals = jnp.sum(weights, axis=-1, keepdims=True)
    softmax_out = (weights / totals).astype(jnp.bfloat16)
    mixed_out = jnp.einsum(
        "shqk,skhd->sqhd", softmax_out, value_rows, preferred_element_type=jnp.float32
    ).astype(jnp.bfloat16)
    return (mixed_out, top_score + jnp.log(totals))


def attend_backward(query_rows, key_rows, value_rows, extra_bias, allowed, log_totals, grad_mixed):
    scores = (
        jnp.einsum("sqhd,skhd->shqk", query_rows, key_rows, preferred_element_type=jnp.float32)
        + extra_bias
    )
    scores = jnp.where(allowed, scores, masked_score)
    softmax_out = jnp.exp(scores - log_totals)
    grad_values = jnp.einsum(
        "shqk,sqhd->skhd",
        softmax_out.astype(jnp.bfloat16),
        grad_mixed,
        preferred_element_type=jnp.float32,
    ).astype(jnp.bfloat16)
    grad_probs = jnp.einsum(
        "sqhd,skhd->shqk", grad_mixed, value_rows, preferred_element_type=jnp.float32
    )
    row_dots = jnp.sum(grad_probs * softmax_out, axis=-1, keepdims=True)
    grad_scores = (softmax_out * (grad_probs - row_dots)).astype(jnp.bfloat16)
    grad_queries = jnp.einsum(
        "shqk,skhd->sqhd", grad_scores, key_rows, preferred_element_type=jnp.float32
    ).astype(jnp.bfloat16)
    grad_keys = jnp.einsum(
        "shqk,sqhd->skhd", grad_scores, query_rows, preferred_element_type=jnp.float32
    ).astype(jnp.bfloat16)
    return (grad_queries, grad_keys, grad_values, grad_scores)


def local(
    block_in,
    enc_states,
    dec_len,
    enc_len,
    gain_self,
    self_query,
    self_key,
    self_value,
    self_out,
    rel_table,
    gain_cross,
    cross_query,
    cross_key,
    cross_value,
    cross_out,
    gain_ff,
    ff_in,
    ff_out,
    out_grad,
):
    seq_count = dec_len.shape[0]
    local_heads = rel_table.shape[1]
    head_size = self_query.shape[1] // local_heads

    def heads_view(values, length):
        return values.reshape(seq_count, length, local_heads, head_size)

    def flat_view(values):
        return values.reshape(values.shape[0] * values.shape[1], local_heads * head_size)

    places = jnp.arange(LEN, dtype=jnp.int32)
    causal = places[None, :] <= places[:, None]
    self_allowed = causal[None, None] & (places[None, None, None, :] < dec_len[:, None, None, None])
    enc_places = jnp.arange(ENC, dtype=jnp.int32)
    cross_allowed = enc_places[None, None, None, :] < enc_len[:, None, None, None]
    onehot = bucket_onehot(LEN)
    rel_bias = jnp.einsum(
        "qkb,bh->hqk", onehot, rel_table.astype(jnp.float32), precision=lax.Precision.HIGHEST
    )[None]
    scale_self = gain_self.astype(jnp.float32)
    scale_cross = gain_cross.astype(jnp.float32)
    scale_ff = gain_ff.astype(jnp.float32)
    residual = block_in.astype(jnp.float32)
    full_self = collect_rows(rms_norm(residual, scale_self).astype(jnp.bfloat16))
    query_self = heads_view(matmul(full_self, self_query).astype(jnp.bfloat16), LEN)
    key_self = heads_view(matmul(full_self, self_key).astype(jnp.bfloat16), LEN)
    value_self = heads_view(matmul(full_self, self_value).astype(jnp.bfloat16), LEN)
    mixed_self, logsum_self = attend_forward(
        query_self, key_self, value_self, rel_bias, self_allowed
    )
    mixed_self = flat_view(mixed_self)
    after_self = residual + spread_rows(matmul(mixed_self, self_out))
    full_cross = collect_rows(rms_norm(after_self, scale_cross).astype(jnp.bfloat16))
    query_cross = heads_view(matmul(full_cross, cross_query).astype(jnp.bfloat16), LEN)
    enc_full = lax.all_gather(enc_states, "tensor", axis=0, tiled=True)
    key_flat = matmul(enc_full, cross_key).astype(jnp.bfloat16)
    value_flat = matmul(enc_full, cross_value).astype(jnp.bfloat16)
    key_cross = heads_view(key_flat, ENC)
    value_cross = heads_view(value_flat, ENC)
    mixed_cross, logsum_cross = attend_forward(
        query_cross, key_cross, value_cross, 0.0, cross_allowed
    )
    mixed_cross = flat_view(mixed_cross)
    after_cross = after_self + spread_rows(matmul(mixed_cross, cross_out))
    full_ff = collect_rows(rms_norm(after_cross, scale_ff).astype(jnp.bfloat16))
    pre_act = matmul(full_ff, ff_in)
    hidden = smooth_act(pre_act).astype(jnp.bfloat16)
    block_out = (after_cross + spread_rows(matmul(hidden, ff_out))).astype(jnp.bfloat16)
    grad_top = out_grad.astype(jnp.float32)
    full_grad_ff = collect_rows(out_grad)
    grad_ff_out = inner_rows(hidden, full_grad_ff)
    grad_pre = act_back(pre_act, times_transposed(full_grad_ff, ff_out)).astype(jnp.bfloat16)
    grad_ff_in = inner_rows(full_ff, grad_pre)
    back_values, grad_gain_ff = norm_back(
        after_cross, scale_ff, spread_rows(times_transposed(grad_pre, ff_in))
    )
    grad_after_cross = grad_top + back_values
    full_grad_cross = collect_rows(grad_after_cross.astype(jnp.bfloat16))
    grad_cross_out = inner_rows(mixed_cross, full_grad_cross)
    grad_mixed_cross = heads_view(
        times_transposed(full_grad_cross, cross_out).astype(jnp.bfloat16), LEN
    )
    grad_query, grad_key, grad_value, unused = attend_backward(
        query_cross, key_cross, value_cross, 0.0, cross_allowed, logsum_cross, grad_mixed_cross
    )
    grad_query = flat_view(grad_query)
    grad_key = flat_view(grad_key)
    grad_value = flat_view(grad_value)
    grad_cross_query = inner_rows(full_cross, grad_query)
    grad_cross_key = inner_rows(enc_full, grad_key)
    grad_cross_value = inner_rows(enc_full, grad_value)
    grad_enc = lax.psum_scatter(
        (times_transposed(grad_key, cross_key) + times_transposed(grad_value, cross_value)).astype(
            jnp.bfloat16
        ),
        "tensor",
        scatter_dimension=0,
        tiled=True,
    ).astype(jnp.float32)
    back_values, grad_gain_cross = norm_back(
        after_self, scale_cross, spread_rows(times_transposed(grad_query, cross_query))
    )
    grad_after_self = grad_after_cross + back_values
    full_grad_self = collect_rows(grad_after_self.astype(jnp.bfloat16))
    grad_self_out = inner_rows(mixed_self, full_grad_self)
    grad_mixed_self = heads_view(
        times_transposed(full_grad_self, self_out).astype(jnp.bfloat16), LEN
    )
    grad_query, grad_key, grad_value, grad_scores = attend_backward(
        query_self, key_self, value_self, rel_bias, self_allowed, logsum_self, grad_mixed_self
    )
    grad_rel_table = jnp.einsum(
        "hqk,qkb->bh",
        jnp.sum(grad_scores.astype(jnp.float32), axis=0),
        onehot,
        precision=lax.Precision.HIGHEST,
    )
    grad_query = flat_view(grad_query)
    grad_key = flat_view(grad_key)
    grad_value = flat_view(grad_value)
    grad_self_query = inner_rows(full_self, grad_query)
    grad_self_key = inner_rows(full_self, grad_key)
    grad_self_value = inner_rows(full_self, grad_value)
    grad_normed = (
        times_transposed(grad_query, self_query)
        + times_transposed(grad_key, self_key)
        + times_transposed(grad_value, self_value)
    )
    back_values, grad_gain_self = norm_back(residual, scale_self, spread_rows(grad_normed))
    grad_in = grad_after_self + back_values
    (
        grad_self_query,
        grad_self_key,
        grad_self_value,
        grad_self_out,
        grad_rel_table,
        grad_cross_query,
        grad_cross_key,
        grad_cross_value,
        grad_cross_out,
        grad_ff_in,
        grad_ff_out,
    ) = (
        lax.psum(grad_self_query.astype(jnp.bfloat16), "dp").astype(jnp.float32),
        lax.psum(grad_self_key.astype(jnp.bfloat16), "dp").astype(jnp.float32),
        lax.psum(grad_self_value.astype(jnp.bfloat16), "dp").astype(jnp.float32),
        lax.psum(grad_self_out.astype(jnp.bfloat16), "dp").astype(jnp.float32),
        lax.psum(grad_rel_table.astype(jnp.bfloat16), "dp").astype(jnp.float32),
        lax.psum(grad_cross_query.astype(jnp.bfloat16), "dp").astype(jnp.float32),
        lax.psum(grad_cross_key.astype(jnp.bfloat16), "dp").astype(jnp.float32),
        lax.psum(grad_cross_value.astype(jnp.bfloat16), "dp").astype(jnp.float32),
        lax.psum(grad_cross_out.astype(jnp.bfloat16), "dp").astype(jnp.float32),
        lax.psum(grad_ff_in.astype(jnp.bfloat16), "dp").astype(jnp.float32),
        lax.psum(grad_ff_out.astype(jnp.bfloat16), "dp").astype(jnp.float32),
    )
    grad_gain_self, grad_gain_cross, grad_gain_ff = lax.psum(
        (grad_gain_self, grad_gain_cross, grad_gain_ff), ("dp", "tensor")
    )
    return (
        block_out,
        grad_in,
        grad_enc,
        grad_gain_self,
        grad_self_query,
        grad_self_key,
        grad_self_value,
        grad_self_out,
        grad_rel_table,
        grad_gain_cross,
        grad_cross_query,
        grad_cross_key,
        grad_cross_value,
        grad_cross_out,
        grad_gain_ff,
        grad_ff_in,
        grad_ff_out,
    )


def solution(mesh):
    placed = (
        P(("dp", "tensor"), None),
        P(("dp", "tensor"), None),
        P("dp"),
        P("dp"),
        P(),
        P(None, "tensor"),
        P(None, "tensor"),
        P(None, "tensor"),
        P("tensor", None),
        P(None, "tensor"),
        P(),
        P(None, "tensor"),
        P(None, "tensor"),
        P(None, "tensor"),
        P("tensor", None),
        P(),
        P(None, "tensor"),
        P("tensor", None),
        P(("dp", "tensor"), None),
    )
    return jax.shard_map(
        local,
        mesh=mesh,
        in_specs=placed,
        out_specs=(
            P(("dp", "tensor"), None),
            P(("dp", "tensor"), None),
            P(("dp", "tensor"), None),
            P(),
            P(None, "tensor"),
            P(None, "tensor"),
            P(None, "tensor"),
            P("tensor", None),
            P(None, "tensor"),
            P(),
            P(None, "tensor"),
            P(None, "tensor"),
            P(None, "tensor"),
            P("tensor", None),
            P(),
            P(None, "tensor"),
            P("tensor", None),
        ),
        check_vma=False,
    )
```

profile of v0, /device:TPU:0, one launch (start us, length us, event | category | flops | bytes accessed | tf_op | source)
XLA Modules:
  0.0 1159.5 jit_solution(13267662903418676840)
XLA Ops:
  14.8 11.5 copy.126
  28.5 15.8 %all-gather.8.cloned.1.call-done = bf16[2048,768]{1,0:T(8,128)(2,1)} async-done(((bf16[512,768]{1,0:T(8,128)(2,1)}), bf16[2048,768]{1,0:T(8,128)(2,1)}) %all-gather.8.cloned.1.call-update) | async-done | bytes 3145744 | tf_op jit(solution)/shard_map/all_gather | solution.py:41
  57.8 3.7 fusion.89
  62.4 57.7 %reduce-scatter.8.cloned.1.call-done = f32[512,768]{1,0:T(8,128)} async-done(((f32[2048,768]{1,0:T(8,128)}), f32[512,768]{1,0:T(8,128)}) %reduce-scatter.8.cloned.1.call-update) | async-done | bytes 1572880 | tf_op jit(solution)/shard_map/reduce_scatter | solution.py:45
  123.8 80.0 %all-gather.10.cloned.1.call-done = bf16[8192,768]{1,0:T(8,128)(2,1)} async-done(((bf16[2048,768]{1,0:T(8,128)(2,1)}), bf16[8192,768]{1,0:T(8,128)(2,1)}) %all-gather.10.cloned.1.call-update) | async-done | bytes 12582928 | tf_op jit(solution)/shard_map/all_gather | solution.py:180
  203.9 8.9 convolution_convert_fusion
  212.8 4.0 copy.165
  216.8 4.4 convolution_convert_fusion.1
  221.2 3.9 copy.163
  225.1 9.4 all-gather.12.cloned.1.call-done
  238.0 11.5 select_reduce_fusion
  249.5 11.0 fusion
  260.5 18.0 %fusion.58 = bf16[8,256,3,64]{1,3,2,0:T(8,128)(2,1)S(1)} fusion(f32[8,3,256,1024]{3,2,1,0:T(8,128)} %get-tuple-element.48, f32[8,3,256]{2,1,0:T(4,128)S(1)} %fusion, f32[8,3,256]{2,1,0:T(4,128)S(1)} %get-tuple-element.47, pred[8,1024]{1,0:T(8,128)(4,1)S(1)} %iota_compare_fusion.2, bf16[8,1024,3,64]{1,0,3,2:T(8,128)(2,1)} %bitcast.180), kind=kOutput, calls=%fused_computation.96 | convolution fusion | flops 830865408 | bytes 29155328 | tf_op jit(solution)/shard_map/shqk,skhd->sqhd/dot_general | solution.py:92
  279.5 3.7 fusion.90
  284.0 57.8 %reduce-scatter.10.cloned.1.call-done = f32[512,768]{1,0:T(8,128)} async-done(((f32[2048,768]{1,0:T(8,128)}), f32[512,768]{1,0:T(8,128)}) %reduce-scatter.10.cloned.1.call-update) | async-done | bytes 1572880 | tf_op jit(solution)/shard_map/reduce_scatter | solution.py:45
  345.8 26.0 %all-gather.16.cloned.1.call-done = bf16[2048,768]{1,0:T(8,128)(2,1)} async-done(((bf16[512,768]{1,0:T(8,128)(2,1)}), bf16[2048,768]{1,0:T(8,128)(2,1)}) %all-gather.16.cloned.1.call-update) | async-done | bytes 3145744 | tf_op jit(solution)/shard_map/all_gather | solution.py:41
  371.8 7.6 fusion.91
  379.4 23.1 %all-gather.14.cloned.1.call-done = bf16[2048,768]{1,0:T(8,128)(2,1)} async-done(((bf16[512,768]{1,0:T(8,128)(2,1)}), bf16[2048,768]{1,0:T(8,128)(2,1)}) %all-gather.14.cloned.1.call-update) | async-done | bytes 3145744 | tf_op jit(solution)/shard_map/all_gather | solution.py:41
  402.5 11.8 %fusion.14 = (bf16[2048,768]{1,0:T(8,128)(2,1)S(1)}, f32[2048,768]{1,0:T(8,128)}) fusion(f32[2048,768]{1,0:T(8,128)} %fusion.91, bf16[2048,768]{1,0:T(8,128)(2,1)} %all-gather.14.cloned.1.call-done, bf16[768,768]{1,0:T(8,128)(2,1)S(1)} %copy-done), kind=kOutput, calls=%fused_computation.25 | convolution fusion | flops 2447376384 | bytes 20054016 | tf_op jit(solution)/shard_map/dot_general | solution.py:67
  415.9 4.6 fusion.92
  420.6 58.4 %reduce-scatter.14.cloned.1.call-done = f32[512,768]{1,0:T(8,128)} async-done(((f32[2048,768]{1,0:T(8,128)}), f32[512,768]{1,0:T(8,128)}) %reduce-scatter.14.cloned.1.call-update) | async-done | bytes 1572880 | tf_op jit(solution)/shard_map/reduce_scatter | solution.py:45
  485.0 28.6 %all-gather.18.cloned.1.call-done = bf16[2048,768]{1,0:T(8,128)(2,1)} async-done(((bf16[512,768]{1,0:T(8,128)(2,1)}), bf16[2048,768]{1,0:T(8,128)(2,1)}) %all-gather.18.cloned.1.call-update) | async-done | bytes 3145744 | tf_op jit(solution)/shard_map/all_gather | solution.py:41
  516.9 23.6 %multiply_reduce_fusion = (f32[8,3,256]{2,1,0:T(4,128)S(1)}, f32[8,3,256,1024]{3,2,1,0:T(8,128)}) fusion(f32[8,3,256,1024]{3,2,1,0:T(8,128)} %get-tuple-element.48, f32[8,3,256]{2,1,0:T(4,128)S(1)} %log_add_fusion.1, pred[8,1024]{1,0:T(8,128)(4,1)S(1)} %iota_compare_fusion.2, bf16[8,1024,3,64]{1,0,3,2:T(8,128)(2,1)} %bitcast.181, ...), kind=kOutput, calls=%fused_computation.2 | convolution fusion | flops 830466048 | bytes 54321152 | tf_op jit(solution)/shard_map/sqhd,skhd->shqk/dot_general | solution.py:111
  540.5 21.9 %multiply_convert_fusion = bf16[8,3,256,1024]{3,2,1,0:T(8,128)(2,1)} fusion(f32[8,3,256,1024]{3,2,1,0:T(8,128)} %get-tuple-element.52, f32[8,3,256,1024]{3,2,1,0:T(8,128)} %get-tuple-element.48, f32[8,3,256]{2,1,0:T(4,128)S(1)} %get-tuple-element.51, f32[8,3,256]{2,1,0:T(4,128)S(1)} %log_add_fusion.1, pred[8,1024]{1,0:T(8,128)(4,1)S(1)} %iota_compare_fusion.2), kind=kLoop, calls=%fused_computation.1 | loop fusion | flops 31457280 | bytes 62971904 | tf_op jit(solution)/shard_map/convert_element_type | solution.py:115
  562.4 10.4 fusion.53
  575.5 3.7 fusion.93
  579.3 10.6 fusion.85
  590.7 7.0 convolution_convert_fusion.9
  597.8 7.3 convolution_convert_fusion.8
  605.1 32.7 %reduce-scatter.16.cloned.1.call-done = f32[512,768]{1,0:T(8,128)} async-done(((f32[2048,768]{1,0:T(8,128)}), f32[512,768]{1,0:T(8,128)}) %reduce-scatter.16.cloned.1.call-update) | async-done | bytes 1572880 | tf_op jit(solution)/shard_map/reduce_scatter | solution.py:45
  640.3 58.5 %reduce-scatter.12.cloned.1.call-done = f32[512,768]{1,0:T(8,128)} async-done(((f32[2048,768]{1,0:T(8,128)}), f32[512,768]{1,0:T(8,128)}) %reduce-scatter.12.cloned.1.call-update) | async-done | bytes 1572880 | tf_op jit(solution)/shard_map/reduce_scatter | solution.py:45
  698.8 5.6 fusion.86
  704.4 11.3 convert_bitcast_fusion
  719.7 8.1 convert_bitcast_fusion.1
  736.7 3.6 fusion.62
  747.2 4.0 fusion.49
  751.2 4.4 multiply_reduce_fusion.1
  755.6 5.7 convert_reduce_fusion
  772.7 13.9 %fusion.96 = f32[8192,768]{1,0:T(8,128)} fusion(bf16[8192,192]{0,1:T(8,128)(2,1)} %bitcast.179, bf16[768,192]{0,1:T(8,128)(2,1)S(1)} %copy-done.35), kind=kOutput, calls=%fused_computation.154 | convolution fusion | flops 2415919104 | bytes 28606464 | tf_op jit(solution)/shard_map/dot_general | solution.py:77
  786.6 14.6 %add_convert_fusion = bf16[8192,768]{1,0:T(8,128)(2,1)} fusion(f32[8192,768]{1,0:T(8,128)} %fusion.96, bf16[8192,192]{0,1:T(8,128)(2,1)} %bitcast.177, bf16[768,192]{0,1:T(8,128)(2,1)S(1)} %copy-done.37), kind=kOutput, calls=%fused_computation | convolution fusion | flops 2428502016 | bytes 41189376 | tf_op jit(solution)/shard_map/dot_general | solution.py:77
  804.4 3.8 add_add_fusion
  809.4 4.1 fusion.63
  813.5 22.4 %psum.103 = bf16[32,3]{0,1:T(4,128)(2,1)S(1)} all-reduce(bf16[32,3]{0,1:T(4,128)(2,1)S(1)} %fusion.63), channel_id=1, replica_groups=mesh['dp'=8,'tensor'=4] {'dp'}, use_global_device_ids=true, to_apply=%region_27.28 | all-reduce | flops 96 | bytes 384 | tf_op jit(solution)/shard_map/psum | solution.py:273
  836.5 108.9 %all-reduce.4.cloned.1.call-done = (bf16[768,192]{0,1:T(8,128)(2,1)}, bf16[768,192]{0,1:T(8,128)(2,1)}, bf16[768,192]{0,1:T(8,128)(2,1)}, bf16[192,768]{1,0:T(8,...) async-done(((bf16[768,192]{0,1:T(8,128)(2,1)}, ...) | async-done | bytes 4718608 | tf_op jit(solution)/shard_map/psum | solution.py:269
  959.5 86.4 %reduce-scatter.20.cloned.1.call-done = bf16[2048,768]{1,0:T(8,128)(2,1)} async-done(((bf16[8192,768]{1,0:T(8,128)(2,1)}), bf16[2048,768]{1,0:T(8,128)(2,1)}) %reduce-scatter.20.cloned.1.call-update) | async-done | bytes 3145744 | tf_op jit(solution)/shard_map/reduce_scatter | solution.py:217
  1045.9 5.1 convert_element_type.260
  1050.9 55.8 %reduce-scatter.18.cloned.1.call-done = f32[512,768]{1,0:T(8,128)} async-done(((f32[2048,768]{1,0:T(8,128)}), f32[512,768]{1,0:T(8,128)}) %reduce-scatter.18.cloned.1.call-update) | async-done | bytes 1572880 | tf_op jit(solution)/shard_map/reduce_scatter | solution.py:45
  1110.1 39.7 %all-reduce = (f32[768]{0:T(1024)}, f32[768]{0:T(1024)}, f32[768]{0:T(1024)}) all-reduce(f32[768]{0:T(1024)} %get-tuple-element.21, f32[768]{0:T(1024)} %get-tuple-element.19, f32[768]{0:T(1024)S(1)} %copy-done.77), channel_id=1, replica_groups=mesh['dp'=8,'tensor'=4] {'dp','tensor'}, use_global_device_ids=true, to_apply=%region_21.22 | all-reduce | flops 2304 | bytes 18432 | tf_op jit(solution)/shard_map/psum | solution.py:281
  (303 shorter events, 109.7 us)
Async XLA Ops:
  7.2 395.3 %copy-start = (bf16[768,768]{1,0:T(8,128)(2,1)S(1)}, bf16[768,768]{1,0:T(8,128)(2,1)}, u32[]{:S(2)}) copy-start(bf16[768,768]{1,0:T(8,128)(2,1)} %param.36) | copy-start | bytes 3538948
  7.2 37.0 %all-gather.8.cloned.1.call-start = ((), (), s32[]{:S(2)}) async-start(), calls=%async_computation.7 | async-start | bytes 3932160 | tf_op jit(solution)/shard_map/all_gather | solution.py:41
  12.9 107.2 %reduce-scatter.8.cloned.1.call-start = ((), (), s32[]{:S(2)}) async-start(), calls=%async_computation.8 | async-start | bytes 7864320 | tf_op jit(solution)/shard_map/reduce_scatter | solution.py:45
  13.6 12.7 %copy-start.80 = (bf16[32,3]{0,1:T(4,128)(2,1)S(1)}, bf16[32,3]{0,1:T(4,128)(2,1)}, u32[]{:S(2)}) copy-start(bf16[32,3]{0,1:T(4,128)(2,1)} %param.29) | copy-start | bytes 580
  26.3 17.9 %copy-start.49 = (bf16[768,192]{0,1:T(8,128)(2,1)S(1)}, bf16[768,192]{0,1:T(8,128)(2,1)}, u32[]{:S(2)}) copy-start(bf16[768,192]{0,1:T(8,128)(2,1)} %param.26) | copy-start | bytes 884740
  28.4 19.2 %copy-start.47 = (bf16[768,192]{0,1:T(8,128)(2,1)S(1)}, bf16[768,192]{0,1:T(8,128)(2,1)}, u32[]{:S(2)}) copy-start(bf16[768,192]{0,1:T(8,128)(2,1)} %param.25) | copy-start | bytes 884740
  61.6 58.5 %copy-start.9 = (bf16[512,768]{1,0:T(8,128)(2,1)S(1)}, bf16[512,768]{1,0:T(8,128)(2,1)}, u32[]{:S(2)}) copy-start(bf16[512,768]{1,0:T(8,128)(2,1)} %param.20) | copy-start | bytes 2359300
  61.6 142.3 %all-gather.10.cloned.1.call-start = ((), (), s32[]{:S(2)}) async-start(), calls=%async_computation.9 | async-start | bytes 15728640 | tf_op jit(solution)/shard_map/all_gather | solution.py:180
  62.3 172.2 %all-gather.12.cloned.1.call-start = ((), (), s32[]{:S(2)}) async-start(), calls=%async_computation.10 | async-start | bytes 3932160 | tf_op jit(solution)/shard_map/all_gather | solution.py:41
  62.4 61.0 %copy-start.61 = (f32[768]{0:T(1024)}, f32[768]{0:T(1024)S(1)}, u32[]{:S(2)}) copy-start(f32[768]{0:T(1024)S(1)} %convert_element_type.226) | copy-start | bytes 9220
  62.4 61.3 %copy-start.83 = (s32[8]{0:T(128)S(1)}, s32[8]{0:T(128)}, u32[]{:S(2)}) copy-start(s32[8]{0:T(128)} %param.23) | copy-start | bytes 100
  122.4 90.4 %copy-start.67 = (f32[512]{0:T(512)}, f32[512]{0:T(512)S(1)}, u32[]{:S(2)}) copy-start(f32[512]{0:T(512)S(1)} %fusion.79) | copy-start | bytes 6148
  123.5 218.3 %reduce-scatter.10.cloned.1.call-start = ((), (), s32[]{:S(2)}) async-start(), calls=%async_computation.11 | async-start | bytes 7864320 | tf_op jit(solution)/shard_map/reduce_scatter | solution.py:45
  203.9 12.9 %copy-start.84 = (bf16[8192,768]{1,0:T(8,128)(2,1)S(1)}, bf16[8192,768]{1,0:T(8,128)(2,1)}, u32[]{:S(2)}) copy-start(bf16[8192,768]{1,0:T(8,128)(2,1)} %all-gather.10.cloned.1.call-done) | copy-start | bytes 37748740
  237.9 11.5 copy-start.22
  249.4 11.1 copy-start.40
  260.5 18.1 %copy-start.59 = (f32[8,3,256]{2,1,0:T(4,128)}, f32[8,3,256]{2,1,0:T(4,128)S(1)}, u32[]{:S(2)}) copy-start(f32[8,3,256]{2,1,0:T(4,128)S(1)} %fusion) | copy-start | bytes 73732
  283.3 88.5 %all-gather.16.cloned.1.call-start = ((), (), s32[]{:S(2)}) async-start(), calls=%async_computation.14 | async-start | bytes 3932160 | tf_op jit(solution)/shard_map/all_gather | solution.py:41
  283.9 118.6 %all-gather.14.cloned.1.call-start = ((), (), s32[]{:S(2)}) async-start(), calls=%async_computation.12 | async-start | bytes 3932160 | tf_op jit(solution)/shard_map/all_gather | solution.py:41
  345.7 133.3 %reduce-scatter.14.cloned.1.call-start = ((), (), s32[]{:S(2)}) async-start(), calls=%async_computation.15 | async-start | bytes 7864320 | tf_op jit(solution)/shard_map/reduce_scatter | solution.py:45
  420.5 61.6 %copy-start.76 = (f32[512]{0:T(512)S(1)}, f32[512]{0:T(512)}, u32[]{:S(2)}) copy-start(f32[512]{0:T(512)} %copy-done.75) | copy-start | bytes 6148
  420.5 61.6 %copy-start.17 = (bf16[512,768]{1,0:T(8,128)(2,1)S(1)}, bf16[512,768]{1,0:T(8,128)(2,1)}, u32[]{:S(2)}) copy-start(bf16[512,768]{1,0:T(8,128)(2,1)} %param.38) | copy-start | bytes 2359300
  420.5 93.1 %all-gather.18.cloned.1.call-start = ((), (), s32[]{:S(2)}) async-start(), calls=%async_computation.16 | async-start | bytes 3932160 | tf_op jit(solution)/shard_map/all_gather | solution.py:41
  482.1 31.6 %copy-start.43 = (bf16[192,768]{1,0:T(8,128)(2,1)S(1)}, bf16[192,768]{1,0:T(8,128)(2,1)}, u32[]{:S(2)}) copy-start(bf16[192,768]{1,0:T(8,128)(2,1)} %param.34) | copy-start | bytes 884740
  484.9 152.9 %reduce-scatter.16.cloned.1.call-start = ((), (), s32[]{:S(2)}) async-start(), calls=%async_computation.17 | async-start | bytes 7864320 | tf_op jit(solution)/shard_map/reduce_scatter | solution.py:45
  540.4 21.9 %copy-start.4 = (bf16[24,8,8,1024]{3,2,1,0:T(8,128)(2,1)S(1)}, bf16[24,8,8,1024]{3,2,1,0:T(8,128)(2,1)}, u32[]{:S(2)}) copy-start(bf16[24,8,8,1024]{3,2,1,0:T(8,128)(2,1)} %copy.165) | copy-start | bytes 9437188
  579.3 119.5 %reduce-scatter.12.cloned.1.call-start = ((), (), s32[]{:S(2)}) async-start(), calls=%async_computation.13 | async-start | bytes 7864320 | tf_op jit(solution)/shard_map/reduce_scatter | solution.py:45
  589.9 153.8 %all-gather.20.cloned.1.call-start = ((), (), s32[]{:S(2)}) async-start(), calls=%async_computation.18 | async-start | bytes 3932160 | tf_op jit(solution)/shard_map/all_gather | solution.py:41
  597.8 40.0 %copy-start.62 = (f32[768]{0:T(1024)S(1)}, f32[768]{0:T(1024)}, u32[]{:S(2)}) copy-start(f32[768]{0:T(1024)} %copy-done.61) | copy-start | bytes 9220
  597.8 40.0 %copy-start.68 = (f32[512]{0:T(512)S(1)}, f32[512]{0:T(512)}, u32[]{:S(2)}) copy-start(f32[512]{0:T(512)} %copy-done.67) | copy-start | bytes 6148
  605.1 35.1 %copy-start.70 = (f32[512]{0:T(512)S(1)}, f32[512]{0:T(512)}, u32[]{:S(2)}) copy-start(f32[512]{0:T(512)} %copy-done.69) | copy-start | bytes 6148
  605.1 93.6 %copy-start.72 = (f32[512]{0:T(512)S(1)}, f32[512]{0:T(512)}, u32[]{:S(2)}) copy-start(f32[512]{0:T(512)} %copy-done.71) | copy-start | bytes 6148
  704.3 241.0 %all-reduce.4.cloned.1.call-start = ((), (), s32[]{:S(2)}) async-start(), calls=%async_computation.21 | async-start | bytes 9437184 | tf_op jit(solution)/shard_map/psum | solution.py:269
  715.7 21.0 %slice-start.2 = ((s8[12582912]{0:T(1024)(128)(4,1)}), s8[4194304]{0:T(1024)(128)(4,1)S(1)}, s32[]{:S(2)}) async-start(s8[12582912]{0:T(1024)(128)(4,1)} %bitcast.222), calls=%async_computation.24 | async-start | bytes 8388608
  719.6 17.0 %copy-start.8 = (bf16[24,8,8,1024]{3,1,2,0:T(8,128)(2,1)}, bf16[24,8,8,1024]{3,1,2,0:T(8,128)(2,1)S(1)}, u32[]{:S(2)}) copy-start(bf16[24,8,8,1024]{3,1,2,0:T(8,128)(2,1)S(1)} %copy.174) | copy-start | bytes 9437188
  719.6 17.0 %slice-start.3 = ((s8[12582912]{0:T(1024)(128)(4,1)}), s8[4194304]{0:T(1024)(128)(4,1)S(1)}, s32[]{:S(2)}) async-start(s8[12582912]{0:T(1024)(128)(4,1)} %bitcast.222), calls=%async_computation.25 | async-start | bytes 8388608
  771.8 14.8 %copy-start.37 = (bf16[768,192]{0,1:T(8,128)(2,1)S(1)}, bf16[768,192]{0,1:T(8,128)(2,1)}, u32[]{:S(2)}) copy-start(bf16[768,192]{0,1:T(8,128)(2,1)} %param.33) | copy-start | bytes 884740
  771.8 274.1 %reduce-scatter.20.cloned.1.call-start = ((), (), s32[]{:S(2)}) async-start(), calls=%async_computation.20 | async-start | bytes 15728640 | tf_op jit(solution)/shard_map/reduce_scatter | solution.py:217
  801.3 305.5 %reduce-scatter.18.cloned.1.call-start = ((), (), s32[]{:S(2)}) async-start(), calls=%async_computation.19 | async-start | bytes 7864320 | tf_op jit(solution)/shard_map/reduce_scatter | solution.py:45
  945.4 9.2 copy-start.52
  945.4 10.1 copy-start.51
  959.5 147.3 %copy-start.10 = (bf16[512,768]{1,0:T(8,128)(2,1)S(1)}, bf16[512,768]{1,0:T(8,128)(2,1)}, u32[]{:S(2)}) copy-start(bf16[512,768]{1,0:T(8,128)(2,1)} %param.20) | copy-start | bytes 2359300
  959.5 147.3 %copy-start.64 = (f32[768]{0:T(1024)S(1)}, f32[768]{0:T(1024)}, u32[]{:S(2)}) copy-start(f32[768]{0:T(1024)} %copy-done.63) | copy-start | bytes 9220
  959.5 147.3 %copy-start.66 = (f32[512]{0:T(512)S(1)}, f32[512]{0:T(512)}, u32[]{:S(2)}) copy-start(f32[512]{0:T(512)} %copy-done.65) | copy-start | bytes 6148
  959.5 150.1 %copy-start.74 = (f32[512]{0:T(512)S(1)}, f32[512]{0:T(512)}, u32[]{:S(2)}) copy-start(f32[512]{0:T(512)} %copy-done.73) | copy-start | bytes 6148
  959.5 150.7 %copy-start.77 = (f32[768]{0:T(1024)S(1)}, f32[768]{0:T(1024)}, u32[]{:S(2)}) copy-start(f32[768]{0:T(1024)} %get-tuple-element.17) | copy-start | bytes 9220
  1106.8 43.1 %copy-start.24 = (f32[512,768]{1,0:T(8,128)S(1)}, f32[512,768]{1,0:T(8,128)}, u32[]{:S(2)}) copy-start(f32[512,768]{1,0:T(8,128)} %reduce-scatter.18.cloned.1.call-done) | copy-start | bytes 4718596
  1106.8 46.0 %copy-start.1 = (bf16[768,768]{1,0:T(8,128)(2,1)S(1)}, bf16[768,768]{1,0:T(8,128)(2,1)}, u32[]{:S(2)}) copy-start(bf16[768,768]{1,0:T(8,128)(2,1)} %param.36) | copy-start | bytes 3538948
  (59 other events, 166.4 us)
Sparse Core Ops, SparseCore 0:
  13.0 31.2 all-gather.7
  61.7 58.3 reduce-scatter.7
  121.7 82.0 all-gather.9
  205.9 28.5 all-gather.11
  283.4 58.3 reduce-scatter.9
  343.2 28.5 all-gather.15
  374.0 28.5 all-gather.13
  420.6 58.3 reduce-scatter.13
  485.1 28.5 all-gather.17
  579.4 58.3 reduce-scatter.15
  640.4 58.3 reduce-scatter.11
  704.5 28.5 all-gather.19
  771.9 173.4 all-reduce.3
  948.0 97.7 reduce-scatter.19
  1048.4 58.3 reduce-scatter.17
where the time goes:
time: 1170 us; the launch traced here: 1160 us
  waiting for transfers between devices  701 us (60%)
  matrix products  240 us (21%)
  other arithmetic  92 us (8%)
  blocking collectives  62.1 us (5%)
  local copies, waits for them, and re-layouts  48.1 us (4%)
  between operations  15.3 us (1%)
    reduce_scatter x6, waiting for transfers between devices, spread_rows(): return lax.psum_scatter(values, 'tensor', scatter_dimension=0, tiled=True)  321 us
    psum x1, waiting for transfers between devices, local(): lax.psum(grad_self_query.astype(jnp.bfloat16), 'dp').astype(jnp.float32)  109 us
    all_gather x6, waiting for transfers between devices, collect_rows(): return lax.all_gather(values, 'tensor', axis=0, tiled=True)  103 us
    reduce_scatter x1, waiting for transfers between devices, local(): lax.psum_scatter((times_transposed(grad_key, cross_key) + times_transpose...  86.4 us
    all_gather x1, waiting for transfers between devices, local(): enc_full = lax.all_gather(enc_states, 'tensor', axis=0, tiled=True)  80 us
    dot_general x10, matrix products, times_transposed(): lax.dot_general(former, latter, (((1,), (1,)), ((), ())), preferred_eleme...  56.5 us
    dot_general x10, matrix products, matmul(): return jnp.dot(former, latter, preferred_element_type=jnp.float32)  51.9 us
    psum x1, blocking collectives, local(): lax.psum((grad_gain_self, grad_gain_cross, grad_gain_ff), ('dp', 'tensor'))  39.7 us
  transfers between devices with their start and end apart: 15, of which 14 were waited for; matrix products, arithmetic and copies ran while one was open for 15% of the time, Pallas kernels for 0%

commit v1 on v0

--- a/solution.py
+++ b/solution.py
@@ -266,7 +266,9 @@
         grad_ff_in,
         grad_ff_out,
     ) = (
-        lax.psum(grad_self_query.astype(jnp.bfloat16), "dp").astype(jnp.float32),
+        jnp.sum(lax.all_gather(grad_self_query.astype(jnp.bfloat16), "dp"), axis=0).astype(
+            jnp.float32
+        ),
         lax.psum(grad_self_key.astype(jnp.bfloat16), "dp").astype(jnp.float32),
         lax.psum(grad_self_value.astype(jnp.bfloat16), "dp").astype(jnp.float32),
         lax.psum(grad_self_out.astype(jnp.bfloat16), "dp").astype(jnp.float32),

time: 1170 us -> 1200 us (1.026)
  waiting for transfers between devices: 701 us -> 725 us
    reduce_scatter x6, waiting for transfers between devices: 321 us -> 336 us  [spread_rows(): return lax.psum_scatter(values, 'tensor', scatter_dimension=0, tiled=True)]
    unnamed x200 -> x219, local copies, waits for them, and re-layouts: 28.9 us -> 31.6 us
  transfers between devices with their start and end apart: 15 -> 16, of which waited for: 14 -> 14; matrix products, arithmetic and copies ran while one was open for 15% -> 16% of each run, Pallas kernels for 0% -> 0%
where the time goes in v1:
time: 1200 us; the launch traced here: 1190 us
  waiting for transfers between devices  725 us (60%)
  matrix products  243 us (20%)
  other arithmetic  93.9 us (8%)
  blocking collectives  62.5 us (5%)
  local copies, waits for them, and re-layouts  52.6 us (4%)
  between operations  15.4 us (1%)
    reduce_scatter x6, waiting for transfers between devices, spread_rows(): return lax.psum_scatter(values, 'tensor', scatter_dimension=0, tiled=True)  336 us
    psum x1, waiting for transfers between devices, local(): lax.psum(grad_self_key.astype(jnp.bfloat16), 'dp').astype(jnp.float32)  117 us
    all_gather x6, waiting for transfers between devices, collect_rows(): return lax.all_gather(values, 'tensor', axis=0, tiled=True)  103 us
    reduce_scatter x1, waiting for transfers between devices, local(): lax.psum_scatter((times_transposed(grad_key, cross_key) + times_transpose...  87.3 us
    all_gather x1, waiting for transfers between devices, local(): enc_full = lax.all_gather(enc_states, 'tensor', axis=0, tiled=True)  80.1 us
    dot_general x10, matrix products, times_transposed(): lax.dot_general(former, latter, (((1,), (1,)), ((), ())), preferred_eleme...  56.1 us
    dot_general x10, matrix products, matmul(): return jnp.dot(former, latter, preferred_element_type=jnp.float32)  51.9 us
    psum x1, blocking collectives, local(): lax.psum((grad_gain_self, grad_gain_cross, grad_gain_ff), ('dp', 'tensor'))  39.7 us
  transfers between devices with their start and end apart: 16, of which 14 were waited for; matrix products, arithmetic and copies ran while one was open for 16% of the time, Pallas kernels for 0%

profile of v1, /device:TPU:0, one launch (start us, length us, event | category | flops | bytes accessed | tf_op | source)
XLA Modules:
  0.0 1194.2 jit_solution(7783508767220800190)
XLA Ops:
  14.8 11.5 copy.126
  28.8 15.5 %all-gather.10.cloned.1.call-done = bf16[2048,768]{1,0:T(8,128)(2,1)} async-done(((bf16[512,768]{1,0:T(8,128)(2,1)}), bf16[2048,768]{1,0:T(8,128)(2,1)}) %all-gather.10.cloned.1.call-update) | async-done | bytes 3145744 | tf_op jit(solution)/shard_map/all_gather | solution.py:41
  57.8 3.7 fusion.89
  62.4 57.7 %reduce-scatter.8.cloned.1.call-done = f32[512,768]{1,0:T(8,128)} async-done(((f32[2048,768]{1,0:T(8,128)}), f32[512,768]{1,0:T(8,128)}) %reduce-scatter.8.cloned.1.call-update) | async-done | bytes 1572880 | tf_op jit(solution)/shard_map/reduce_scatter | solution.py:45
  123.8 80.1 %all-gather.12.cloned.1.call-done = bf16[8192,768]{1,0:T(8,128)(2,1)} async-done(((bf16[2048,768]{1,0:T(8,128)(2,1)}), bf16[8192,768]{1,0:T(8,128)(2,1)}) %all-gather.12.cloned.1.call-update) | async-done | bytes 12582928 | tf_op jit(solution)/shard_map/all_gather | solution.py:180
  203.9 8.9 convolution_convert_fusion
  212.8 3.8 copy.165
  216.6 4.4 convolution_convert_fusion.1
  221.0 3.9 copy.163
  224.9 9.6 all-gather.14.cloned.1.call-done
  237.9 11.5 select_reduce_fusion
  249.5 11.0 fusion
  260.5 18.0 %fusion.58 = bf16[8,256,3,64]{1,3,2,0:T(8,128)(2,1)S(1)} fusion(f32[8,3,256,1024]{3,2,1,0:T(8,128)} %get-tuple-element.47, f32[8,3,256]{2,1,0:T(4,128)S(1)} %fusion, f32[8,3,256]{2,1,0:T(4,128)S(1)} %get-tuple-element.46, pred[8,1024]{1,0:T(8,128)(4,1)S(1)} %iota_compare_fusion.2, bf16[8,1024,3,64]{1,0,3,2:T(8,128)(2,1)} %bitcast.189), kind=kOutput, calls=%fused_computation.97 | convolution fusion | flops 830865408 | bytes 29155328 | tf_op jit(solution)/shard_map/shqk,skhd->sqhd/dot_general | solution.py:92
  279.5 3.7 fusion.90
  284.0 57.9 %reduce-scatter.10.cloned.1.call-done = f32[512,768]{1,0:T(8,128)} async-done(((f32[2048,768]{1,0:T(8,128)}), f32[512,768]{1,0:T(8,128)}) %reduce-scatter.10.cloned.1.call-update) | async-done | bytes 1572880 | tf_op jit(solution)/shard_map/reduce_scatter | solution.py:45
  345.8 26.0 %all-gather.18.cloned.1.call-done = bf16[2048,768]{1,0:T(8,128)(2,1)} async-done(((bf16[512,768]{1,0:T(8,128)(2,1)}), bf16[2048,768]{1,0:T(8,128)(2,1)}) %all-gather.18.cloned.1.call-update) | async-done | bytes 3145744 | tf_op jit(solution)/shard_map/all_gather | solution.py:41
  371.8 7.6 fusion.91
  379.4 23.1 %all-gather.16.cloned.1.call-done = bf16[2048,768]{1,0:T(8,128)(2,1)} async-done(((bf16[512,768]{1,0:T(8,128)(2,1)}), bf16[2048,768]{1,0:T(8,128)(2,1)}) %all-gather.16.cloned.1.call-update) | async-done | bytes 3145744 | tf_op jit(solution)/shard_map/all_gather | solution.py:41
  402.5 11.7 fusion.14
  415.9 4.5 fusion.92
  420.6 58.4 %reduce-scatter.14.cloned.1.call-done = f32[512,768]{1,0:T(8,128)} async-done(((f32[2048,768]{1,0:T(8,128)}), f32[512,768]{1,0:T(8,128)}) %reduce-scatter.14.cloned.1.call-update) | async-done | bytes 1572880 | tf_op jit(solution)/shard_map/reduce_scatter | solution.py:45
  485.0 28.6 %all-gather.20.cloned.1.call-done = bf16[2048,768]{1,0:T(8,128)(2,1)} async-done(((bf16[512,768]{1,0:T(8,128)(2,1)}), bf16[2048,768]{1,0:T(8,128)(2,1)}) %all-gather.20.cloned.1.call-update) | async-done | bytes 3145744 | tf_op jit(solution)/shard_map/all_gather | solution.py:41
  516.9 23.2 %multiply_reduce_fusion = (f32[8,3,256]{2,1,0:T(4,128)S(1)}, f32[8,3,256,1024]{3,2,1,0:T(8,128)}) fusion(f32[8,3,256,1024]{3,2,1,0:T(8,128)} %get-tuple-element.47, f32[8,3,256]{2,1,0:T(4,128)S(1)} %log_add_fusion.1, pred[8,1024]{1,0:T(8,128)(4,1)S(1)} %iota_compare_fusion.2, bf16[8,1024,3,64]{1,0,3,2:T(8,128)(2,1)} %bitcast.190, ...), kind=kOutput, calls=%fused_computation.2 | convolution fusion | flops 830466048 | bytes 54321152 | tf_op jit(solution)/shard_map/sqhd,skhd->shqk/dot_general | solution.py:111
  540.1 21.9 %multiply_convert_fusion = bf16[8,3,256,1024]{3,2,1,0:T(8,128)(2,1)} fusion(f32[8,3,256,1024]{3,2,1,0:T(8,128)} %get-tuple-element.51, f32[8,3,256,1024]{3,2,1,0:T(8,128)} %get-tuple-element.47, f32[8,3,256]{2,1,0:T(4,128)S(1)} %get-tuple-element.50, f32[8,3,256]{2,1,0:T(4,128)S(1)} %log_add_fusion.1, pred[8,1024]{1,0:T(8,128)(4,1)S(1)} %iota_compare_fusion.2), kind=kLoop, calls=%fused_computation.1 | loop fusion | flops 31457280 | bytes 62971904 | tf_op jit(solution)/shard_map/convert_element_type | solution.py:115
  562.0 10.4 fusion.53
  575.1 3.7 fusion.93
  578.9 10.6 fusion.85
  589.6 47.8 %reduce-scatter.16.cloned.1.call-done = f32[512,768]{1,0:T(8,128)} async-done(((f32[2048,768]{1,0:T(8,128)}), f32[512,768]{1,0:T(8,128)}) %reduce-scatter.16.cloned.1.call-update) | async-done | bytes 1572880 | tf_op jit(solution)/shard_map/reduce_scatter | solution.py:45
  639.9 58.5 %reduce-scatter.12.cloned.1.call-done = f32[512,768]{1,0:T(8,128)} async-done(((f32[2048,768]{1,0:T(8,128)}), f32[512,768]{1,0:T(8,128)}) %reduce-scatter.12.cloned.1.call-update) | async-done | bytes 1572880 | tf_op jit(solution)/shard_map/reduce_scatter | solution.py:45
  698.3 5.6 fusion.86
  704.4 6.7 convolution_convert_fusion.9
  711.1 7.8 convolution_convert_fusion.8
  718.9 3.9 convert_bitcast_fusion.1
  722.8 12.5 %convert_bitcast_fusion = bf16[8,1024,3,64]{1,3,2,0:T(8,128)(2,1)} fusion(f32[8,3,256,1024]{3,2,1,0:T(8,128)} %get-tuple-element.47, f32[8,3,256]{2,1,0:T(4,128)S(1)} %log_add_fusion.1, pred[8,1024]{1,0:T(8,128)(4,1)S(1)} %iota_compare_fusion.2, bf16[8,256,3,64]{1,0,3,2:T(8,128)(2,1)S(1)} %bitcast.194), kind=kOutput, calls=%fused_computation.39 | convolution fusion | flops 825753600 | bytes 29130752 | tf_op jit(solution)/shard_map/shqk,sqhd->skhd/dot_general | solution.py:105
  738.7 7.3 multiply_reduce_fusion.1
  746.1 5.6 convert_reduce_fusion
  771.7 8.1 fusion.62
  779.8 3.9 fusion.61
  794.3 13.8 %fusion.96 = f32[8192,768]{1,0:T(8,128)} fusion(bf16[8192,192]{0,1:T(8,128)(2,1)} %bitcast.188, bf16[768,192]{0,1:T(8,128)(2,1)S(1)} %copy-done.40), kind=kOutput, calls=%fused_computation.155 | convolution fusion | flops 2415919104 | bytes 28606464 | tf_op jit(solution)/shard_map/dot_general | solution.py:77
  808.1 14.5 %add_convert_fusion = bf16[8192,768]{1,0:T(8,128)(2,1)} fusion(f32[8192,768]{1,0:T(8,128)} %fusion.96, bf16[8192,192]{0,1:T(8,128)(2,1)} %bitcast.186, bf16[768,192]{0,1:T(8,128)(2,1)S(1)} %copy-done.42), kind=kOutput, calls=%fused_computation | convolution fusion | flops 2428502016 | bytes 41189376 | tf_op jit(solution)/shard_map/dot_general | solution.py:77
  825.7 3.8 add_add_fusion
  830.7 4.1 fusion.63
  834.8 22.8 %psum.95 = bf16[32,3]{0,1:T(4,128)(2,1)S(1)} all-reduce(bf16[32,3]{0,1:T(4,128)(2,1)S(1)} %fusion.63), channel_id=1, replica_groups=mesh['dp'=8,'tensor'=4] {'dp'}, use_global_device_ids=true, to_apply=%region_27.28 | all-reduce | flops 96 | bytes 384 | tf_op jit(solution)/shard_map/psum | solution.py:275
  863.0 117.0 %all-reduce.4.cloned.1.call-done = (bf16[768,192]{0,1:T(8,128)(2,1)}, bf16[768,192]{0,1:T(8,128)(2,1)}, bf16[192,768]{1,0:T(8,128)(2,1)}, bf16[768,192]{0,1:T(8,...) async-done(((bf16[768,192]{0,1:T(8,128)(2,1)}, ...) | async-done | bytes 4423696 | tf_op jit(solution)/shard_map/psum | solution.py:272
  993.2 87.3 %reduce-scatter.20.cloned.1.call-done = bf16[2048,768]{1,0:T(8,128)(2,1)} async-done(((bf16[8192,768]{1,0:T(8,128)(2,1)}), bf16[2048,768]{1,0:T(8,128)(2,1)}) %reduce-scatter.20.cloned.1.call-update) | async-done | bytes 3145744 | tf_op jit(solution)/shard_map/reduce_scatter | solution.py:217
  1080.5 5.1 convert_element_type.262
  1085.5 55.9 %reduce-scatter.18.cloned.1.call-done = f32[512,768]{1,0:T(8,128)} async-done(((f32[2048,768]{1,0:T(8,128)}), f32[512,768]{1,0:T(8,128)}) %reduce-scatter.18.cloned.1.call-update) | async-done | bytes 1572880 | tf_op jit(solution)/shard_map/reduce_scatter | solution.py:45
  1144.8 39.7 %all-reduce = (f32[768]{0:T(1024)}, f32[768]{0:T(1024)}, f32[768]{0:T(1024)}) all-reduce(f32[768]{0:T(1024)} %get-tuple-element.21, f32[768]{0:T(1024)} %get-tuple-element.19, f32[768]{0:T(1024)S(1)} %copy-done.81), channel_id=1, replica_groups=mesh['dp'=8,'tensor'=4] {'dp','tensor'}, use_global_device_ids=true, to_apply=%region_21.22 | all-reduce | flops 2304 | bytes 18432 | tf_op jit(solution)/shard_map/psum | solution.py:283
  (328 shorter events, 116.2 us)
Async XLA Ops:
  7.2 395.3 %copy-start = (bf16[768,768]{1,0:T(8,128)(2,1)S(1)}, bf16[768,768]{1,0:T(8,128)(2,1)}, u32[]{:S(2)}) copy-start(bf16[768,768]{1,0:T(8,128)(2,1)} %param.36) | copy-start | bytes 3538948
  7.2 37.0 %all-gather.10.cloned.1.call-start = ((), (), s32[]{:S(2)}) async-start(), calls=%async_computation.7 | async-start | bytes 3932160 | tf_op jit(solution)/shard_map/all_gather | solution.py:41
  12.9 107.2 %reduce-scatter.8.cloned.1.call-start = ((), (), s32[]{:S(2)}) async-start(), calls=%async_computation.8 | async-start | bytes 7864320 | tf_op jit(solution)/shard_map/reduce_scatter | solution.py:45
  13.6 12.7 %copy-start.84 = (bf16[32,3]{0,1:T(4,128)(2,1)S(1)}, bf16[32,3]{0,1:T(4,128)(2,1)}, u32[]{:S(2)}) copy-start(bf16[32,3]{0,1:T(4,128)(2,1)} %param.29) | copy-start | bytes 580
  26.3 17.9 %copy-start.54 = (bf16[768,192]{0,1:T(8,128)(2,1)S(1)}, bf16[768,192]{0,1:T(8,128)(2,1)}, u32[]{:S(2)}) copy-start(bf16[768,192]{0,1:T(8,128)(2,1)} %param.26) | copy-start | bytes 884740
  28.8 18.9 %copy-start.52 = (bf16[768,192]{0,1:T(8,128)(2,1)S(1)}, bf16[768,192]{0,1:T(8,128)(2,1)}, u32[]{:S(2)}) copy-start(bf16[768,192]{0,1:T(8,128)(2,1)} %param.25) | copy-start | bytes 884740
  61.6 58.5 %copy-start.12 = (bf16[512,768]{1,0:T(8,128)(2,1)S(1)}, bf16[512,768]{1,0:T(8,128)(2,1)}, u32[]{:S(2)}) copy-start(bf16[512,768]{1,0:T(8,128)(2,1)} %param.20) | copy-start | bytes 2359300
  61.6 142.3 %all-gather.12.cloned.1.call-start = ((), (), s32[]{:S(2)}) async-start(), calls=%async_computation.9 | async-start | bytes 15728640 | tf_op jit(solution)/shard_map/all_gather | solution.py:180
  62.3 172.2 %all-gather.14.cloned.1.call-start = ((), (), s32[]{:S(2)}) async-start(), calls=%async_computation.10 | async-start | bytes 3932160 | tf_op jit(solution)/shard_map/all_gather | solution.py:41
  62.4 61.0 %copy-start.65 = (f32[768]{0:T(1024)}, f32[768]{0:T(1024)S(1)}, u32[]{:S(2)}) copy-start(f32[768]{0:T(1024)S(1)} %convert_element_type.228) | copy-start | bytes 9220
  62.4 61.3 %copy-start.87 = (s32[8]{0:T(128)S(1)}, s32[8]{0:T(128)}, u32[]{:S(2)}) copy-start(s32[8]{0:T(128)} %param.23) | copy-start | bytes 100
  122.3 90.4 %copy-start.71 = (f32[512]{0:T(512)}, f32[512]{0:T(512)S(1)}, u32[]{:S(2)}) copy-start(f32[512]{0:T(512)S(1)} %fusion.79) | copy-start | bytes 6148
  123.5 218.4 %reduce-scatter.10.cloned.1.call-start = ((), (), s32[]{:S(2)}) async-start(), calls=%async_computation.11 | async-start | bytes 7864320 | tf_op jit(solution)/shard_map/reduce_scatter | solution.py:45
  203.9 12.8 %copy-start.88 = (bf16[8192,768]{1,0:T(8,128)(2,1)S(1)}, bf16[8192,768]{1,0:T(8,128)(2,1)}, u32[]{:S(2)}) copy-start(bf16[8192,768]{1,0:T(8,128)(2,1)} %all-gather.12.cloned.1.call-done) | copy-start | bytes 37748740
  260.5 18.1 %copy-start.63 = (f32[8,3,256]{2,1,0:T(4,128)}, f32[8,3,256]{2,1,0:T(4,128)S(1)}, u32[]{:S(2)}) copy-start(f32[8,3,256]{2,1,0:T(4,128)S(1)} %fusion) | copy-start | bytes 73732
  283.3 88.5 %all-gather.18.cloned.1.call-start = ((), (), s32[]{:S(2)}) async-start(), calls=%async_computation.14 | async-start | bytes 3932160 | tf_op jit(solution)/shard_map/all_gather | solution.py:41
  283.9 118.6 %all-gather.16.cloned.1.call-start = ((), (), s32[]{:S(2)}) async-start(), calls=%async_computation.12 | async-start | bytes 3932160 | tf_op jit(solution)/shard_map/all_gather | solution.py:41
  345.8 133.2 %reduce-scatter.14.cloned.1.call-start = ((), (), s32[]{:S(2)}) async-start(), calls=%async_computation.15 | async-start | bytes 7864320 | tf_op jit(solution)/shard_map/reduce_scatter | solution.py:45
  420.5 61.6 %copy-start.80 = (f32[512]{0:T(512)S(1)}, f32[512]{0:T(512)}, u32[]{:S(2)}) copy-start(f32[512]{0:T(512)} %copy-done.79) | copy-start | bytes 6148
  420.5 61.6 %copy-start.21 = (bf16[512,768]{1,0:T(8,128)(2,1)S(1)}, bf16[512,768]{1,0:T(8,128)(2,1)}, u32[]{:S(2)}) copy-start(bf16[512,768]{1,0:T(8,128)(2,1)} %param.38) | copy-start | bytes 2359300
  420.5 93.1 %all-gather.20.cloned.1.call-start = ((), (), s32[]{:S(2)}) async-start(), calls=%async_computation.16 | async-start | bytes 3932160 | tf_op jit(solution)/shard_map/all_gather | solution.py:41
  482.0 31.6 %copy-start.48 = (bf16[192,768]{1,0:T(8,128)(2,1)S(1)}, bf16[192,768]{1,0:T(8,128)(2,1)}, u32[]{:S(2)}) copy-start(bf16[192,768]{1,0:T(8,128)(2,1)} %param.34) | copy-start | bytes 884740
  484.9 152.5 %reduce-scatter.16.cloned.1.call-start = ((), (), s32[]{:S(2)}) async-start(), calls=%async_computation.17 | async-start | bytes 7864320 | tf_op jit(solution)/shard_map/reduce_scatter | solution.py:45
  540.1 21.9 %copy-start.4 = (bf16[24,8,8,1024]{3,2,1,0:T(8,128)(2,1)S(1)}, bf16[24,8,8,1024]{3,2,1,0:T(8,128)(2,1)}, u32[]{:S(2)}) copy-start(bf16[24,8,8,1024]{3,2,1,0:T(8,128)(2,1)} %copy.165) | copy-start | bytes 9437188
  578.9 119.5 %reduce-scatter.12.cloned.1.call-start = ((), (), s32[]{:S(2)}) async-start(), calls=%async_computation.13 | async-start | bytes 7864320 | tf_op jit(solution)/shard_map/reduce_scatter | solution.py:45
  589.5 47.9 %copy-start.66 = (f32[768]{0:T(1024)S(1)}, f32[768]{0:T(1024)}, u32[]{:S(2)}) copy-start(f32[768]{0:T(1024)} %copy-done.65) | copy-start | bytes 9220
  589.5 47.9 %copy-start.72 = (f32[512]{0:T(512)S(1)}, f32[512]{0:T(512)}, u32[]{:S(2)}) copy-start(f32[512]{0:T(512)} %copy-done.71) | copy-start | bytes 6148
  589.5 50.3 %copy-start.74 = (f32[512]{0:T(512)S(1)}, f32[512]{0:T(512)}, u32[]{:S(2)}) copy-start(f32[512]{0:T(512)} %copy-done.73) | copy-start | bytes 6148
  589.5 108.8 %copy-start.76 = (f32[512]{0:T(512)S(1)}, f32[512]{0:T(512)}, u32[]{:S(2)}) copy-start(f32[512]{0:T(512)} %copy-done.75) | copy-start | bytes 6148
  589.5 145.8 %all-gather.22.cloned.1.call-start = ((), (), s32[]{:S(2)}) async-start(), calls=%async_computation.18 | async-start | bytes 3932160 | tf_op jit(solution)/shard_map/all_gather | solution.py:41
  639.8 64.5 %copy-start.44 = (f32[8,3,256]{2,1,0:T(4,128)S(1)}, f32[8,3,256]{2,1,0:T(4,128)}, u32[]{:S(2)}) copy-start(f32[8,3,256]{2,1,0:T(4,128)} %copy-done.43) | copy-start | bytes 73732
  639.8 64.5 %copy-start.62 = (f32[8,3,256]{2,1,0:T(4,128)S(1)}, f32[8,3,256]{2,1,0:T(4,128)}, u32[]{:S(2)}) copy-start(f32[8,3,256]{2,1,0:T(4,128)} %copy-done.61) | copy-start | bytes 73732
  703.9 154.3 %all-gather.24.cloned.1.call-start = ((), (), s32[]{:S(2)}) async-start(), calls=%async_computation.21 | async-start | bytes 2654208 | tf_op jit(solution)/shard_map/all_gather | solution.py:269
  704.4 14.5 %slice-start = ((s8[12582912]{0:T(1024)(128)(4,1)}), s8[4194304]{0:T(1024)(128)(4,1)S(1)}, s32[]{:S(2)}) async-start(s8[12582912]{0:T(1024)(128)(4,1)} %bitcast.177), calls=%async_computation.23 | async-start | bytes 8388608
  722.8 12.5 %copy-start.51 = (bf16[192,768]{1,0:T(8,128)(2,1)S(1)}, bf16[192,768]{1,0:T(8,128)(2,1)}, u32[]{:S(2)}) copy-start(bf16[192,768]{1,0:T(8,128)(2,1)} %param.28) | copy-start | bytes 884740
  756.3 223.7 %all-reduce.4.cloned.1.call-start = ((), (), s32[]{:S(2)}) async-start(), calls=%async_computation.22 | async-start | bytes 8847360 | tf_op jit(solution)/shard_map/psum | solution.py:272
  767.6 12.2 %slice-start.7 = ((s8[12582912]{0:T(1024)(128)(4,1)}), s8[4194304]{0:T(1024)(128)(4,1)S(1)}, s32[]{:S(2)}) async-start(s8[12582912]{0:T(1024)(128)(4,1)} %bitcast.232), calls=%async_computation.30 | async-start | bytes 8388608
  771.7 12.0 %slice-start.5 = ((s8[6291456]{0:T(1024)(128)(4,1)}), s8[4194304]{0:T(1024)(128)(4,1)S(1)}, s32[]{:S(2)}) async-start(s8[6291456]{0:T(1024)(128)(4,1)} %bitcast.181), calls=%async_computation.28 | async-start | bytes 8388608
  793.4 14.7 %copy-start.42 = (bf16[768,192]{0,1:T(8,128)(2,1)S(1)}, bf16[768,192]{0,1:T(8,128)(2,1)}, u32[]{:S(2)}) copy-start(bf16[768,192]{0,1:T(8,128)(2,1)} %param.33) | copy-start | bytes 884740
  793.4 287.1 %reduce-scatter.20.cloned.1.call-start = ((), (), s32[]{:S(2)}) async-start(), calls=%async_computation.20 | async-start | bytes 15728640 | tf_op jit(solution)/shard_map/reduce_scatter | solution.py:217
  822.6 318.8 %reduce-scatter.18.cloned.1.call-start = ((), (), s32[]{:S(2)}) async-start(), calls=%async_computation.19 | async-start | bytes 7864320 | tf_op jit(solution)/shard_map/reduce_scatter | solution.py:45
  993.2 148.3 %copy-start.13 = (bf16[512,768]{1,0:T(8,128)(2,1)S(1)}, bf16[512,768]{1,0:T(8,128)(2,1)}, u32[]{:S(2)}) copy-start(bf16[512,768]{1,0:T(8,128)(2,1)} %param.20) | copy-start | bytes 2359300
  993.2 148.3 %copy-start.68 = (f32[768]{0:T(1024)S(1)}, f32[768]{0:T(1024)}, u32[]{:S(2)}) copy-start(f32[768]{0:T(1024)} %copy-done.67) | copy-start | bytes 9220
  993.2 148.3 %copy-start.70 = (f32[512]{0:T(512)S(1)}, f32[512]{0:T(512)}, u32[]{:S(2)}) copy-start(f32[512]{0:T(512)} %copy-done.69) | copy-start | bytes 6148
  993.2 151.0 %copy-start.78 = (f32[512]{0:T(512)S(1)}, f32[512]{0:T(512)}, u32[]{:S(2)}) copy-start(f32[512]{0:T(512)} %copy-done.77) | copy-start | bytes 6148
  993.2 151.6 %copy-start.81 = (f32[768]{0:T(1024)S(1)}, f32[768]{0:T(1024)}, u32[]{:S(2)}) copy-start(f32[768]{0:T(1024)} %get-tuple-element.17) | copy-start | bytes 9220
  1141.4 43.1 %copy-start.30 = (f32[512,768]{1,0:T(8,128)S(1)}, f32[512,768]{1,0:T(8,128)}, u32[]{:S(2)}) copy-start(f32[512,768]{1,0:T(8,128)} %reduce-scatter.18.cloned.1.call-done) | copy-start | bytes 4718596
  1141.4 46.0 %copy-start.1 = (bf16[768,768]{1,0:T(8,128)(2,1)S(1)}, bf16[768,768]{1,0:T(8,128)(2,1)}, u32[]{:S(2)}) copy-start(bf16[768,768]{1,0:T(8,128)(2,1)} %param.36) | copy-start | bytes 3538948
  (69 other events, 252.9 us)
Sparse Core Ops, SparseCore 0:
  13.0 31.2 all-gather.9
  61.7 58.3 reduce-scatter.7
  121.7 82.0 all-gather.11
  205.9 28.5 all-gather.13
  283.4 58.3 reduce-scatter.9
  343.3 28.5 all-gather.17
  374.0 28.5 all-gather.15
  420.6 58.3 reduce-scatter.13
  485.0 28.5 all-gather.19
  579.0 58.3 reduce-scatter.15
  639.9 58.3 reduce-scatter.11
  704.0 28.5 all-gather.21
  756.4 52.2 all-gather.23
  815.8 164.1 all-reduce.3
  982.6 97.7 reduce-scatter.19
  1083.0 58.3 reduce-scatter.17
